TPU v7x, 32 devices: a whole 2x2x4 slice. The times are simulated.
32 devices in a mesh: grp: 4 (over y, x), seq: 8 (over z, core).
Axes of the slice: x: 2, y: 2, z: 4, core: 2. Of those that a mesh axis runs over, the one named last changes fastest.
Arguments:
- tokens: bfloat16 [4096, 2048], P(('grp', 'seq')), may hold values from -6.6 to 6.6
- grad_output: bfloat16 [4096, 2048], P(('grp', 'seq')), may hold values from -6 to 6
- query_gain: float32 [2048], replicated, may hold values from -6 to 6
- key_gain: float32 [2048], replicated, may hold values from -6 to 6
- short_query_gain: float32 [2048], replicated, may hold values from -24 to 24
- short_key_gain: float32 [2048], replicated, may hold values from -24 to 24
Outputs:
- grad_tokens: bfloat16 [4096, 2048], P(('grp', 'seq'))
- gain_grads: float32 [4, 2048], replicated
All inputs are finite; a program needn't handle non-finite values.
Results may differ from a plain program's by a relative error of at most 0.019.
Values may be sent and summed in bfloat16 or wider, within the bound.
No kernel may reach another device: no remote copies, remote signals or barrier semaphores. Data moves between devices by JAX's collectives and lax.ppermute only.
A program may use at most 64 MiB of HBM per device.

v0:
```python
import jax
import jax.numpy as jnp
from jax import lax
from jax.sharding import PartitionSpec as P

HEADS = 16
WINDOW = 128
SHORTEN = 16


NEGATIVE = -1e30


def shifted_2(value, axis, steps):
    count = lax.axis_size(axis)
    leading, last = (max(0, -steps), min(count, count - steps))
    return lax.ppermute(value, axis, [(source, source + steps) for source in range(leading, last)])


def head_scores(queries, key_rows):
    temper = queries.shape[-1] ** (-0.5)
    return (
        jnp.einsum("qhe,khe->hqk", queries, key_rows, preferred_element_type=jnp.float32) * temper
    )


def short_order(absolute, block_rows, group_rows, seq_count):
    within = absolute % group_rows
    source = absolute // group_rows
    return (within // block_rows * seq_count + source) * block_rows + within % block_rows


def shards(tokens, grad_output, query_gain, key_gain, short_query_gain, short_key_gain):
    local_rows, model_width = tokens.shape
    head_size = model_width // HEADS
    temper = head_size ** (-0.5)
    chain_index = lax.axis_index(("grp", "seq"))
    token_f = tokens.astype(jnp.float32)
    query_heads = (token_f * query_gain).astype(jnp.bfloat16).reshape(local_rows, HEADS, head_size)
    prior_rows = shifted_2(tokens, ("grp", "seq"), 1)
    context = jnp.concatenate([prior_rows, tokens], axis=0)
    context_f = context.astype(jnp.float32)
    key_heads = (
        (context_f * key_gain).astype(jnp.bfloat16).reshape(local_rows + WINDOW, HEADS, head_size)
    )
    value_heads = context.reshape(local_rows + WINDOW, HEADS, head_size)
    query_pos = chain_index * local_rows + jnp.arange(local_rows, dtype=jnp.int32)[:, None]
    key_pos = (
        chain_index * local_rows
        - WINDOW
        + jnp.arange(local_rows + WINDOW, dtype=jnp.int32)[None, :]
    )
    allowed = (key_pos <= query_pos) & (key_pos > query_pos - WINDOW) & (key_pos >= 0)
    scores = jnp.where(allowed[None], head_scores(query_heads, key_heads), NEGATIVE)
    log_total = jax.nn.logsumexp(scores, axis=-1)
    weights = jnp.where(allowed[None], jnp.exp(scores - log_total[..., None]), 0.0)
    weights_low = weights.astype(jnp.bfloat16)
    local_out = jnp.einsum(
        "hqk,khe->qhe", weights_low, value_heads, preferred_element_type=jnp.float32
    ).reshape(local_rows, model_width)
    mixed_rows = (token_f + local_out).astype(jnp.bfloat16)
    tail_rows = shifted_2(mixed_rows[local_rows - (SHORTEN - 1) :], ("grp", "seq"), 1)
    shifted = jnp.concatenate([tail_rows, mixed_rows], axis=0)[:local_rows]
    short_rows = local_rows // SHORTEN
    pooled = (
        shifted.astype(jnp.float32).reshape(short_rows, SHORTEN, model_width).sum(axis=1)
        * (1.0 / SHORTEN)
    ).astype(jnp.bfloat16)
    grad_short = (
        grad_output.astype(jnp.float32)
        .reshape(short_rows, SHORTEN, model_width)
        .sum(axis=1)
        .astype(jnp.bfloat16)
    )
    groups = lax.axis_size("grp")
    seq_count = lax.axis_size("seq")
    group_index = lax.axis_index("grp")
    seq_index = lax.axis_index("seq")
    head_width = model_width // groups
    head_part = head_width // head_size
    group_rows = short_rows * groups
    pooled_here, grad_here = (
        lax.all_to_all(
            pooled.reshape(short_rows, groups, head_width),
            "grp",
            split_axis=1,
            concat_axis=0,
            tiled=True,
        ),
        lax.all_to_all(
            grad_short.reshape(short_rows, groups, head_width),
            "grp",
            split_axis=1,
            concat_axis=0,
            tiled=True,
        ),
    )
    pooled_here = pooled_here.reshape(group_rows, head_width)
    grad_here = grad_here.reshape(group_rows, head_width)
    gain_query = lax.dynamic_slice_in_dim(short_query_gain, group_index * head_width, head_width)
    gain_key = lax.dynamic_slice_in_dim(short_key_gain, group_index * head_width, head_width)
    pooled_f = pooled_here.astype(jnp.float32)
    short_queries = (
        (pooled_f * gain_query).astype(jnp.bfloat16).reshape(group_rows, head_part, head_size)
    )
    short_keys = (
        (pooled_f * gain_key).astype(jnp.bfloat16).reshape(group_rows, head_part, head_size)
    )
    short_values = pooled_here.reshape(group_rows, head_part, head_size)
    short_incoming = grad_here.reshape(group_rows, head_part, head_size)
    own_pos = short_order(
        seq_index * group_rows + jnp.arange(group_rows, dtype=jnp.int32),
        short_rows,
        group_rows,
        seq_count,
    )
    peak = jnp.full((head_part, group_rows), NEGATIVE, jnp.float32)
    fetched_keys = lax.all_gather(short_keys, "seq", axis=0, tiled=True)
    fetched_values = lax.all_gather(short_values, "seq", axis=0, tiled=True)
    remote_pos = short_order(
        jnp.arange(fetched_keys.shape[0], dtype=jnp.int32), short_rows, group_rows, seq_count
    )
    visible = remote_pos[None, :] <= own_pos[:, None]
    piece_scores = jnp.where(visible[None], head_scores(short_queries, fetched_keys), NEGATIVE)
    highest = jnp.maximum(peak, piece_scores.max(axis=-1))
    piece_weights = jnp.where(visible[None], jnp.exp(piece_scores - highest[..., None]), 0.0)
    piece_grads = jnp.einsum(
        "qhe,khe->hqk", short_incoming, fetched_values, preferred_element_type=jnp.float32
    )
    total_sum = piece_weights.sum(axis=-1)
    weighted_sum = (piece_weights * piece_grads).sum(axis=-1)
    short_log_total = highest + jnp.log(total_sum)
    short_dot = weighted_sum / total_sum
    fetched_keys = lax.all_gather(short_keys, "seq", axis=0, tiled=True)
    fetched_values = lax.all_gather(short_values, "seq", axis=0, tiled=True)
    remote_pos = short_order(
        jnp.arange(fetched_keys.shape[0], dtype=jnp.int32), short_rows, group_rows, seq_count
    )
    visible = remote_pos[None, :] <= own_pos[:, None]
    piece_weights = jnp.where(
        visible[None],
        jnp.exp(head_scores(short_queries, fetched_keys) - short_log_total[..., None]),
        0.0,
    )
    piece_grads = jnp.einsum(
        "qhe,khe->hqk", short_incoming, fetched_values, preferred_element_type=jnp.float32
    )
    piece_ds = (piece_weights * (piece_grads - short_dot[..., None])).astype(jnp.bfloat16)
    short_gq = (
        jnp.einsum("hqk,khe->qhe", piece_ds, fetched_keys, preferred_element_type=jnp.float32)
        * temper
    )
    stats_all, dots_all = (
        lax.all_gather(short_log_total.T, "seq", axis=0, tiled=True),
        lax.all_gather(short_dot.T, "seq", axis=0, tiled=True),
    )
    fetched_queries = lax.all_gather(short_queries, "seq", axis=0, tiled=True)
    fetched_incoming = lax.all_gather(short_incoming, "seq", axis=0, tiled=True)
    count = fetched_queries.shape[0]
    remote_pos = short_order(jnp.arange(count, dtype=jnp.int32), short_rows, group_rows, seq_count)
    visible = own_pos[None, :] <= remote_pos[:, None]
    remote_total = stats_all.T
    remote_dot = dots_all.T
    piece_weights = jnp.where(
        visible[None],
        jnp.exp(head_scores(fetched_queries, short_keys) - remote_total[..., None]),
        0.0,
    )
    piece_grads = jnp.einsum(
        "qhe,khe->hqk", fetched_incoming, short_values, preferred_element_type=jnp.float32
    )
    piece_ds = (piece_weights * (piece_grads - remote_dot[..., None])).astype(jnp.bfloat16)
    grad_keys = (
        jnp.einsum("hqk,qhe->khe", piece_ds, fetched_queries, preferred_element_type=jnp.float32)
        * temper
    )
    grad_values = jnp.einsum(
        "hqk,qhe->khe",
        piece_weights.astype(jnp.bfloat16),
        fetched_incoming,
        preferred_element_type=jnp.float32,
    )
    short_gk = grad_keys
    short_gv = grad_values
    short_gq = short_gq.reshape(group_rows, head_width)
    short_gk = short_gk.reshape(group_rows, head_width)
    short_gv = short_gv.reshape(group_rows, head_width)
    grad_pooled_here = (
        grad_here.astype(jnp.float32) + short_gq * gain_query + short_gk * gain_key + short_gv
    )
    empty_width = jnp.zeros((model_width,), jnp.float32)
    grad_short_query = lax.dynamic_update_slice(
        empty_width, jnp.sum(short_gq * pooled_f, axis=0), (group_index * head_width,)
    )
    grad_short_key = lax.dynamic_update_slice(
        empty_width, jnp.sum(short_gk * pooled_f, axis=0), (group_index * head_width,)
    )
    grad_pooled = (
        lax.all_to_all(
            grad_pooled_here.reshape(group_rows, 1, head_width).astype(jnp.bfloat16),
            "grp",
            split_axis=0,
            concat_axis=1,
            tiled=True,
        )
        .astype(jnp.float32)
        .reshape(short_rows, model_width)
    )
    following = shifted_2(grad_pooled[:1], ("grp", "seq"), -1)
    grad_following = jnp.concatenate([grad_pooled[1:], following], axis=0)
    spread = jnp.concatenate(
        [
            grad_pooled[:, None],
            jnp.broadcast_to(grad_following[:, None], (short_rows, SHORTEN - 1, model_width)),
        ],
        axis=1,
    ) * (1.0 / SHORTEN)
    grad_mixed = grad_output.astype(jnp.float32) + spread.reshape(local_rows, model_width)
    incoming_heads = grad_mixed.astype(jnp.bfloat16).reshape(local_rows, HEADS, head_size)
    local_dw = jnp.einsum(
        "qhe,khe->hqk", incoming_heads, value_heads, preferred_element_type=jnp.float32
    )
    local_dot = jnp.sum(weights * local_dw, axis=-1, keepdims=True)
    local_ds = (weights * (local_dw - local_dot)).astype(jnp.bfloat16)
    local_gq = (
        jnp.einsum("hqk,khe->qhe", local_ds, key_heads, preferred_element_type=jnp.float32) * temper
    ).reshape(local_rows, model_width)
    full_gk = (
        jnp.einsum("hqk,qhe->khe", local_ds, query_heads, preferred_element_type=jnp.float32)
        * temper
    ).reshape(local_rows + WINDOW, model_width)
    full_gv = jnp.einsum(
        "hqk,qhe->khe", weights_low, incoming_heads, preferred_element_type=jnp.float32
    ).reshape(local_rows + WINDOW, model_width)
    returned = full_gk[:WINDOW] * key_gain + full_gv[:WINDOW]
    arriving = shifted_2(returned.astype(jnp.bfloat16), ("grp", "seq"), -1).astype(returned.dtype)
    edge_gain = jnp.sum(full_gk[:WINDOW] * context_f[:WINDOW], axis=0)
    local_gk = full_gk[WINDOW:]
    local_gv = full_gv[WINDOW:]
    grad_tokens = grad_mixed + local_gq * query_gain + local_gk * key_gain + local_gv
    grad_tokens = grad_tokens.at[local_rows - WINDOW :].add(arriving)
    grad_query_gain = jnp.sum(local_gq * token_f, axis=0)
    grad_key_gain = jnp.sum(local_gk * token_f, axis=0) + edge_gain
    summed = lax.psum(
        jnp.stack([grad_query_gain, grad_key_gain, grad_short_query, grad_short_key]),
        ("grp", "seq"),
    )
    total_tokens = local_rows * lax.axis_size(("grp", "seq"))
    return (grad_tokens.astype(jnp.bfloat16), summed * total_tokens ** (-0.5))


def solution(mesh):
    return jax.shard_map(
        shards,
        mesh=mesh,
        in_specs=(P(("grp", "seq"), None), P(("grp", "seq"), None), P(), P(), P(), P()),
        out_specs=(P(("grp", "seq"), None), P()),
        check_vma=False,
    )
```

profile of v0, /device:TPU:0, one launch (start us, length us, event | category | flops | bytes accessed | tf_op | source)
XLA Modules:
  0.0 233.8 jit_solution(2646998995256428641)
XLA Ops:
  0.7 1.9 bitcast_reduce_fusion
  2.6 5.2 %all-to-all-start = ((bf16[8,4,512]{2,0,1:T(8,128)(2,1)}), bf16[8,4,512]{2,0,1:T(8,128)(2,1)S(1)}, u32[]{:S(2)}, u32[]{:S(2)}) async-start(bf16[8,4,512]{2,0,1:T(8,128)(2,1)} %bitcast.1), calls=%async_computation | async-start | bytes 65536 | tf_op jit(solution)/shard_map/all_to_all | solution.py:90
  9.3 2.0 copy.116
  16.2 2.1 fusion.49
  21.1 2.6 %copy.87 = f32[128,2048]{1,0:T(8,128)} copy(f32[128,2048]{0,1:T(8,128)} %bitcast.113) | data formatting | bytes 2097152 | tf_op jit(solution)/shard_map/reshape | solution.py:60
  25.1 5.9 %collective-permute-start.1 = (bf16[15,2048]{1,0:T(8,128)(2,1)S(1)}, bf16[15,2048]{1,0:T(8,128)(2,1)S(1)}, u32[]{:S(2)}, u32[]{:S(2)}) collective-permute-start(bf16[15,2048]{1,0:T(8,128)(2,1)S(1)} %slice.78), channel_id=1, source_target_pairs={{0,1},{1,2},{2,3},{3,4},{4,5},{5,6},{6,7},{7,8},{8,9},{9,10},{10,1... | collective-permute-start | bytes 184328 | tf_op jit(solution)/shard_map/ppermute | solution.py:17
  33.3 13.4 %all-to-all-start.1 = ((bf16[8,4,512]{2,0,1:T(8,128)(2,1)}), bf16[8,4,512]{2,0,1:T(8,128)(2,1)S(1)}, u32[]{:S(2)}, u32[]{:S(2)}) async-start(bf16[8,4,512]{2,0,1:T(8,128)(2,1)} %bitcast.12), calls=%async_computation.1 | async-start | bytes 65536 | tf_op jit(solution)/shard_map/all_to_all | solution.py:83
  46.7 14.2 %all_gather.24 = bf16[256,4,128]{2,0,1:T(8,128)(2,1)S(1)} all-gather(bf16[32,4,128]{2,0,1:T(8,128)(2,1)S(1)} %copy.90), channel_id=1, replica_groups=mesh['grp'=4,'seq'=8] {'seq'}, dimensions={0}, use_global_device_ids=true | all-gather | bytes 294912 | tf_op jit(solution)/shard_map/all_gather | solution.py:158
  60.9 14.2 %all_gather.21 = bf16[256,4,128]{2,0,1:T(8,128)(2,1)S(1)} all-gather(bf16[32,4,128]{2,0,1:T(8,128)(2,1)S(1)} %copy.88), channel_id=1, replica_groups=mesh['grp'=4,'seq'=8] {'seq'}, dimensions={0}, use_global_device_ids=true | all-gather | bytes 294912 | tf_op jit(solution)/shard_map/all_gather | solution.py:135
  75.1 14.2 %all_gather.20 = bf16[256,4,128]{2,0,1:T(8,128)(2,1)S(1)} all-gather(bf16[32,4,128]{2,0,1:T(8,128)(2,1)S(1)} %get-tuple-element.37), channel_id=1, replica_groups=mesh['grp'=4,'seq'=8] {'seq'}, dimensions={0}, use_global_device_ids=true | all-gather | bytes 294912 | tf_op jit(solution)/shard_map/all_gather | solution.py:134
  89.4 14.2 %all_gather.22 = bf16[256,4,128]{2,0,1:T(8,128)(2,1)S(1)} all-gather(bf16[32,4,128]{2,0,1:T(8,128)(2,1)S(1)} %get-tuple-element.38), channel_id=1, replica_groups=mesh['grp'=4,'seq'=8] {'seq'}, dimensions={0}, use_global_device_ids=true | all-gather | bytes 294912 | tf_op jit(solution)/shard_map/all_gather | solution.py:157
  106.0 12.8 %all-gather = f32[8,32,4]{1,2,0:T(4,128)S(1)} all-gather(f32[1,32,4]{1,2,0:T(4,128)S(1)} %bitcast.130), channel_id=1, replica_groups=mesh['grp'=4,'seq'=8] {'seq'}, dimensions={0}, use_global_device_ids=true | all-gather | bytes 4608 | tf_op jit(solution)/shard_map/all_gather | solution.py:154
  119.4 12.8 %all-gather.1 = f32[8,32,4]{1,2,0:T(4,128)S(1)} all-gather(f32[1,32,4]{1,2,0:T(4,128)S(1)} %bitcast.129), channel_id=1, replica_groups=mesh['grp'=4,'seq'=8] {'seq'}, dimensions={0}, use_global_device_ids=true | all-gather | bytes 4608 | tf_op jit(solution)/shard_map/all_gather | solution.py:155
  141.6 8.7 %all_to_all.39 = bf16[4,2,2048]{2,1,0:T(2,128)(2,1)S(1)} all-to-all(bf16[4,2,2048]{2,1,0:T(2,128)(2,1)S(1)} %reshape.656), channel_id=1, replica_groups=mesh['grp'=4,'seq'=8] {'grp'}, dimensions={0} | all-to-all | bytes 65536 | tf_op jit(solution)/shard_map/all_to_all | solution.py:199
  155.7 2.0 copy.118
  157.8 3.6 %multiply_reduce_fusion = (f32[16,128]{1,0:T(8,128)S(1)}, f32[16,128,256]{2,1,0:T(8,128)}) fusion(f32[16,128,256]{2,1,0:T(8,128)S(1)} %get-tuple-element.42, f32[16,128]{1,0:T(8,128)S(1)} %log_add_fusion, pred[128,256]{1,0:T(8,128)(4,1)S(1)} %copy-done.16, bf16[128,16,128]{0,2,1:T(8,128)(2,1)} %bitcast.107, bf16[256,16,128]{0,2,1:T(8,128)(2,1)} %bitcast.105), kind=kOutput, calls=%fused_computation.2 | convolution fusion | flops 136312832 | bytes 5816320 | tf_op jit(solution)/shard_map/qhe,khe->hqk/dot_general | solution.py:220
  163.6 2.5 %copy.109 = f32[128,2048]{1,0:T(8,128)} copy(f32[128,2048]{0,1:T(8,128)} %bitcast.111) | data formatting | bytes 2097152 | tf_op jit(solution)/shard_map/slice | solution.py:235
  166.1 2.0 multiply_convert_fusion
  171.2 2.6 %copy.108 = f32[128,2048]{1,0:T(8,128)} copy(f32[128,2048]{0,1:T(8,128)} %bitcast.112) | data formatting | bytes 2097152 | tf_op jit(solution)/shard_map/slice | solution.py:235
  173.9 2.7 %multiply_reduce_fusion.1 = (f32[2048]{0:T(1024)S(1)}, bf16[128,2048]{1,0:T(8,128)(2,1)}) fusion(f32[128,2048]{1,0:T(8,128)} %copy.108, bf16[128,2048]{1,0:T(8,128)(2,1)S(1)} %copy-done.6, f32[128,2048]{1,0:T(8,128)} %copy.109, f32[2048]{0:T(1024)S(1)} %copy-done.24), kind=kLoop, calls=%fused_computation.36 | loop fusion | flops 1570816 | bytes 3162112 | tf_op jit(solution)/shard_map/reduce_sum | solution.py:237
  179.5 2.6 %copy.103 = f32[128,2048]{1,0:T(8,128)} copy(f32[128,2048]{0,1:T(8,128)} %bitcast.116) | data formatting | bytes 2097152 | tf_op jit(solution)/shard_map/reshape | solution.py:227
  183.4 2.6 %copy.105 = f32[128,2048]{1,0:T(8,128)} copy(f32[128,2048]{0,1:T(8,128)} %bitcast.110) | data formatting | bytes 2097152 | tf_op jit(solution)/shard_map/slice | solution.py:238
  186.0 3.0 %fusion.10 = (f32[2048]{0:T(1024)S(1)}, f32[2048]{0:T(1024)S(1)}, bf16[128,2048]{1,0:T(8,128)(2,1)}) fusion(f32[128,2048]{1,0:T(8,128)S(1)} %copy-done.11, bf16[128,2048]{1,0:T(8,128)(2,1)S(1)} %copy-done, f32[128,2048]{1,0:T(8,128)} %copy.105, bf16[128,2048]{1,0:T(8,128)(2,1)} %collective-permute-done.3, f32[128,2048]{1,0:T(8,128)} %copy.107, ...), kind=kLoop, calls=%fused_computation.29 | loop fusion | flops 3928064 | bytes 6324224 | tf_op jit(solution)/shard_map/reduce_sum | solution.py:242
  189.1 44.0 %psum.7 = f32[4,2048]{1,0:T(4,128)S(1)} all-reduce(f32[4,2048]{1,0:T(4,128)S(1)} %pad_maximum_fusion.3), channel_id=1, replica_groups=mesh['grp'=4,'seq'=8] {'grp','seq'}, use_global_device_ids=true, to_apply=%region_13.14 | all-reduce | flops 8192 | bytes 65536 | tf_op jit(solution)/shard_map/psum | solution.py:244
  (141 shorter events, 40.5 us)
Async XLA Ops:
  0.6 13.1 %copy-start = (bf16[128,2048]{1,0:T(8,128)(2,1)S(1)}, bf16[128,2048]{1,0:T(8,128)(2,1)}, u32[]{:S(2)}) copy-start(bf16[128,2048]{1,0:T(8,128)(2,1)} %param.10) | copy-start | bytes 1572868
  0.6 12.1 %copy-start.27 = (f32[2048]{0:T(1024)S(1)}, f32[2048]{0:T(1024)}, u32[]{:S(2)}) copy-start(f32[2048]{0:T(1024)} %param.14) | copy-start | bytes 24580
  2.6 29.8 %all-to-all-start = ((bf16[8,4,512]{2,0,1:T(8,128)(2,1)}), bf16[8,4,512]{2,0,1:T(8,128)(2,1)S(1)}, u32[]{:S(2)}, u32[]{:S(2)}) async-start(bf16[8,4,512]{2,0,1:T(8,128)(2,1)} %bitcast.1), calls=%async_computation | async-start | bytes 65536 | tf_op jit(solution)/shard_map/all_to_all | solution.py:90
  7.7 6.0 %collective-permute-start = (bf16[128,2048]{1,0:T(8,128)(2,1)}, bf16[128,2048]{1,0:T(8,128)(2,1)S(1)}, u32[]{:S(2)}, u32[]{:S(2)}) collective-permute-start(bf16[128,2048]{1,0:T(8,128)(2,1)} %param.10), channel_id=1, source_target_pairs={{0,1},{1,2},{2,3},{3,4},{4,5},{5,6},{6,7},{7,8},{8,9},{9,10},{10,1... | collective-permute-start | bytes 1572872 | tf_op jit(solution)/shard_map/ppermute | solution.py:17
  12.8 3.4 %copy-start.12 = (bf16[128,2048]{0,1:T(8,128)(2,1)}, bf16[128,2048]{0,1:T(8,128)(2,1)S(1)}, u32[]{:S(2)}) copy-start(bf16[128,2048]{0,1:T(8,128)(2,1)S(1)} %copy.117) | copy-start | bytes 1572868
  13.7 5.3 %copy-start.15 = (pred[128,256]{1,0:T(8,128)(4,1)}, pred[128,256]{1,0:T(8,128)(4,1)S(1)}, u32[]{:S(2)}) copy-start(pred[128,256]{1,0:T(8,128)(4,1)S(1)} %and_and_fusion) | copy-start | bytes 98308
  21.1 9.9 %copy-start.28 = (f32[2048]{0:T(1024)S(1)}, f32[2048]{0:T(1024)}, u32[]{:S(2)}) copy-start(f32[2048]{0:T(1024)} %param.15) | copy-start | bytes 24580
  25.1 7.4 %collective-permute-start.1 = (bf16[15,2048]{1,0:T(8,128)(2,1)S(1)}, bf16[15,2048]{1,0:T(8,128)(2,1)S(1)}, u32[]{:S(2)}, u32[]{:S(2)}) collective-permute-start(bf16[15,2048]{1,0:T(8,128)(2,1)S(1)} %slice.78), channel_id=1, source_target_pairs={{0,1},{1,2},{2,3},{3,4},{4,5},{5,6},{6,7},{7,8},{8,9},{9,10},{10,1... | collective-permute-start | bytes 184328 | tf_op jit(solution)/shard_map/ppermute | solution.py:17
  32.4 42.8 %copy-start.21 = (bf16[8,4,512]{2,0,1:T(8,128)(2,1)}, bf16[8,4,512]{2,0,1:T(8,128)(2,1)S(1)}, u32[]{:S(2)}) copy-start(bf16[8,4,512]{2,0,1:T(8,128)(2,1)S(1)} %all-to-all-done) | copy-start | bytes 98308
  33.3 27.6 %all-to-all-start.1 = ((bf16[8,4,512]{2,0,1:T(8,128)(2,1)}), bf16[8,4,512]{2,0,1:T(8,128)(2,1)S(1)}, u32[]{:S(2)}, u32[]{:S(2)}) async-start(bf16[8,4,512]{2,0,1:T(8,128)(2,1)} %bitcast.12), calls=%async_computation.1 | async-start | bytes 65536 | tf_op jit(solution)/shard_map/all_to_all | solution.py:83
  60.8 28.5 %copy-start.17 = (bf16[32,4,128]{2,1,0:T(4,128)(2,1)}, bf16[32,4,128]{2,1,0:T(4,128)(2,1)S(1)}, u32[]{:S(2)}) copy-start(bf16[32,4,128]{2,1,0:T(4,128)(2,1)S(1)} %reshape.640) | copy-start | bytes 98308
  75.1 14.2 %copy-start.20 = (bf16[32,4,128]{2,0,1:T(8,128)(2,1)}, bf16[32,4,128]{2,0,1:T(8,128)(2,1)S(1)}, u32[]{:S(2)}) copy-start(bf16[32,4,128]{2,0,1:T(8,128)(2,1)S(1)} %get-tuple-element.37) | copy-start | bytes 98308
  105.4 27.5 %copy-start.25 = (f32[4,32]{1,0:T(4,128)}, f32[4,32]{1,0:T(4,128)S(1)}, u32[]{:S(2)}) copy-start(f32[4,32]{1,0:T(4,128)S(1)} %get-tuple-element.39) | copy-start | bytes 1540
  140.9 13.9 %copy-start.4 = (bf16[128,2048]{1,0:T(8,128)(2,1)S(1)}, bf16[128,2048]{1,0:T(8,128)(2,1)}, u32[]{:S(2)}) copy-start(bf16[128,2048]{1,0:T(8,128)(2,1)} %param.11) | copy-start | bytes 1572868
  150.5 3.1 %collective-permute-start.2 = (f32[1,2048]{1,0:T(1,128)S(1)}, f32[1,2048]{1,0:T(1,128)S(1)}, u32[]{:S(2)}, u32[]{:S(2)}) collective-permute-start(f32[1,2048]{1,0:T(1,128)S(1)} %bitcast.135), channel_id=1, source_target_pairs={{1,0},{2,1},{3,2},{4,3},{5,4},{6,5},{7,6},{8,7},{9,8},{10,9},{11,1... | collective-permute-start | bytes 24584 | tf_op jit(solution)/shard_map/ppermute | solution.py:17
  157.8 3.6 %copy-start.7 = (bf16[128,2048]{0,1:T(8,128)(2,1)S(1)}, bf16[128,2048]{0,1:T(8,128)(2,1)}, u32[]{:S(2)}) copy-start(bf16[128,2048]{0,1:T(8,128)(2,1)} %copy.118) | copy-start | bytes 1572868
  166.1 3.0 %copy-start.13 = (bf16[128,2048]{0,1:T(8,128)(2,1)S(1)}, bf16[128,2048]{0,1:T(8,128)(2,1)}, u32[]{:S(2)}) copy-start(bf16[128,2048]{0,1:T(8,128)(2,1)} %copy-done.12) | copy-start | bytes 1572868
  173.8 4.1 %copy-start.9 = (bf16[16,128,256]{2,1,0:T(8,128)(2,1)S(1)}, bf16[16,128,256]{2,1,0:T(8,128)(2,1)}, u32[]{:S(2)}) copy-start(bf16[16,128,256]{2,1,0:T(8,128)(2,1)} %copy-done.8) | copy-start | bytes 3145732
  173.8 4.1 %copy-start.18 = (bf16[128,2048]{0,1:T(8,128)(2,1)S(1)}, bf16[128,2048]{0,1:T(8,128)(2,1)}, u32[]{:S(2)}) copy-start(bf16[128,2048]{0,1:T(8,128)(2,1)} %copy.116) | copy-start | bytes 1572868
  173.8 4.1 %copy-start.19 = (bf16[128,2048]{0,1:T(8,128)(2,1)S(1)}, bf16[128,2048]{0,1:T(8,128)(2,1)}, u32[]{:S(2)}) copy-start(bf16[128,2048]{0,1:T(8,128)(2,1)} %copy.115) | copy-start | bytes 1572868
  176.6 9.4 %collective-permute-start.3 = (bf16[128,2048]{1,0:T(8,128)(2,1)}, bf16[128,2048]{1,0:T(8,128)(2,1)}, u32[]{:S(2)}, u32[]{:S(2)}) collective-permute-start(bf16[128,2048]{1,0:T(8,128)(2,1)} %get-tuple-element.34), channel_id=1, source_target_pairs={{1,0},{2,1},{3,2},{4,3},{5,4},{6,5},{7,6},{8,7},{9,8},{10,9},{11,1... | collective-permute-start | bytes 1572872 | tf_op jit(solution)/shard_map/ppermute | solution.py:17
  178.0 4.1 %copy-start.10 = (f32[128,16,128]{0,2,1:T(8,128)S(1)}, f32[128,16,128]{0,2,1:T(8,128)}, u32[]{:S(2)}) copy-start(f32[128,16,128]{0,2,1:T(8,128)} %get-tuple-element.31) | copy-start | bytes 3145732
  182.0 4.0 %copy-start.2 = (f32[8,16,2048]{2,1,0:T(8,128)S(1)}, f32[8,16,2048]{2,1,0:T(8,128)}, u32[]{:S(2)}) copy-start(f32[8,16,2048]{2,1,0:T(8,128)} %copy-done.1) | copy-start | bytes 3145732
  182.0 4.0 %copy-start.22 = (f32[2048]{0:T(1024)S(1)}, f32[2048]{0:T(1024)}, u32[]{:S(2)}) copy-start(f32[2048]{0:T(1024)} %param.12) | copy-start | bytes 24580
  (11 other events, 19.1 us)
where the time goes:
time: 235 us; the launch traced here: 234 us
  blocking collectives  135 us (57%)
  local copies, waits for them, and re-layouts  33.7 us (14%)
  starting transfers between devices  28.7 us (12%)
  other arithmetic  18 us (8%)
  matrix products  15.6 us (7%)
    psum x1, blocking collectives, shards(): lax.psum(jnp.stack([grad_query_gain, grad_key_gain, grad_short_query, gra...  44 us
    all_gather x1, blocking collectives, shards(): fetched_keys = lax.all_gather(short_keys, 'seq', axis=0, tiled=True)  14.2 us
    all_gather x1, blocking collectives, shards(): fetched_values = lax.all_gather(short_values, 'seq', axis=0, tiled=True)  14.2 us
    all_gather x1, blocking collectives, shards(): fetched_queries = lax.all_gather(short_queries, 'seq', axis=0, tiled=True)  14.2 us
    all_gather x1, blocking collectives, shards(): fetched_incoming = lax.all_gather(short_incoming, 'seq', axis=0, tiled=True)  14.2 us
    all_to_all x1, starting transfers between devices, shards(): lax.all_to_all(pooled.reshape(short_rows, groups, head_width), 'grp', spl...  13.4 us
    all_gather x1, blocking collectives, shards(): lax.all_gather(short_log_total.T, 'seq', axis=0, tiled=True)  12.8 us
    all_gather x1, blocking collectives, shards(): lax.all_gather(short_dot.T, 'seq', axis=0, tiled=True)  12.8 us
  transfers between devices with their start and end apart: 6, of which 1 were waited for; matrix products, arithmetic and copies ran while one was open for 11% of the time, Pallas kernels for 0%

commit v1 on v0

--- a/solution.py
+++ b/solution.py
@@ -1,6 +1,10 @@
+import functools
+
 import jax
 import jax.numpy as jnp
 from jax import lax
+from jax.experimental import pallas as pl
+from jax.experimental.pallas import tpu as pltpu
 from jax.sharding import PartitionSpec as P
 
 HEADS = 16
@@ -9,12 +13,283 @@
 
 
 NEGATIVE = -1e30
+CHAIN = ("grp", "seq")
+TILE = 8
+COPIES = 2
 
 
 def shifted_2(value, axis, steps):
     count = lax.axis_size(axis)
     leading, last = (max(0, -steps), min(count, count - steps))
     return lax.ppermute(value, axis, [(source, source + steps) for source in range(leading, last)])
+
+
+def mm(a, b):
+    return lax.dot_general(a, b, (((1,), (0,)), ((), ())), preferred_element_type=jnp.float32)
+
+
+def mm_nt(a, b):
+    return lax.dot_general(a, b, (((1,), (1,)), ((), ())), preferred_element_type=jnp.float32)
+
+
+def mm_tn(a, b):
+    return lax.dot_general(a, b, (((0,), (0,)), ((), ())), preferred_element_type=jnp.float32)
+
+
+def iotas(rows, columns):
+    return (
+        lax.broadcasted_iota(jnp.int32, (rows, columns), 0),
+        lax.broadcasted_iota(jnp.int32, (rows, columns), 1),
+    )
+
+
+def chain_index():
+    return lax.axis_index("grp") * lax.axis_size("seq") + lax.axis_index("seq")
+
+
+def own_kernel(tokens, grad_output, gains, out, peak, total, grad_short):
+    rows, width = tokens.shape
+    size = width // HEADS
+    temper = size ** (-0.5)
+    q_pos, k_pos = iotas(rows, rows)
+    allowed = k_pos <= q_pos
+    short, row = iotas(rows // SHORTEN, rows)
+    pool = (row // SHORTEN == short).astype(jnp.bfloat16)
+    lane = lax.broadcasted_iota(jnp.int32, (rows, size), 1)
+    peaks = jnp.zeros((rows, size), jnp.float32)
+    totals = jnp.zeros((rows, size), jnp.float32)
+    for head in range(HEADS):
+        part = slice(head * size, (head + 1) * size)
+        low = tokens[:, part]
+        x = low.astype(jnp.float32)
+        q = (x * gains[0:1, part]).astype(jnp.bfloat16)
+        k = (x * gains[1:2, part]).astype(jnp.bfloat16)
+        scores = jnp.where(allowed, mm_nt(q, k) * temper, NEGATIVE)
+        high = jnp.max(scores, axis=1, keepdims=True)
+        weights = jnp.exp(scores - high)
+        out[:, part] = mm(weights.astype(jnp.bfloat16), low)
+        peaks = jnp.where(lane == head, high, peaks)
+        totals = jnp.where(lane == head, jnp.sum(weights, axis=1, keepdims=True), totals)
+        grad_short[head] = mm(pool, grad_output[:, part]).astype(jnp.bfloat16)
+    peak[...] = peaks
+    total[...] = totals
+
+
+def prior_kernel(tokens, prior, gains, out, peak, total, grad_short, send):
+    rows, width = tokens.shape
+    size = width // HEADS
+    temper = size ** (-0.5)
+    q_pos, k_pos = iotas(rows, rows)
+    allowed = (k_pos > q_pos) & (chain_index() > 0)
+    short, row = iotas(2 * TILE, rows)
+    pool = ((row + SHORTEN - 1) // SHORTEN == short).astype(jnp.bfloat16)
+    tile_row = lax.broadcasted_iota(jnp.int32, (TILE, size), 0)
+    for head in range(HEADS):
+        part = slice(head * size, (head + 1) * size)
+        x = tokens[:, part].astype(jnp.float32)
+        low = prior[:, part]
+        q = (x * gains[0:1, part]).astype(jnp.bfloat16)
+        k = (low.astype(jnp.float32) * gains[1:2, part]).astype(jnp.bfloat16)
+        scores = jnp.where(allowed, mm_nt(q, k) * temper, NEGATIVE)
+        own_high = peak[:, head : head + 1]
+        high = jnp.maximum(jnp.max(scores, axis=1, keepdims=True), own_high)
+        weights = jnp.exp(scores - high)
+        fade = jnp.exp(own_high - high)
+        sums = total[:, head : head + 1] * fade + jnp.sum(weights, axis=1, keepdims=True)
+        local = (out[:, part] * fade + mm(weights.astype(jnp.bfloat16), low)) / sums
+        mixed = (x + local).astype(jnp.bfloat16)
+        pooled = mm(pool, mixed)
+        rows_sent = jnp.where(tile_row == 0, pooled[:TILE], pooled[:TILE] * (1.0 / SHORTEN))
+        tail = pooled[TILE:]
+        tail_high = tail.astype(jnp.bfloat16).astype(jnp.float32)
+        tail_low = pltpu.roll(tail - tail_high, 1, 0)
+        tail_rows = jnp.where(tile_row == 0, tail_high, tail_low)
+        for copy in range(COPIES):
+            send[head * COPIES + copy, 0:TILE, :] = rows_sent.astype(jnp.bfloat16)
+            send[head * COPIES + copy, TILE : 2 * TILE, :] = tail_rows.astype(jnp.bfloat16)
+            send[head * COPIES + copy, 2 * TILE : 3 * TILE, :] = grad_short[head]
+
+
+def short_kernel(received, gains, send):
+    count, _, size = received.shape
+    rows = count * TILE
+    temper = size ** (-0.5)
+    me = chain_index()
+    head = me // COPIES
+    copy = me % COPIES
+    gain_q = gains[pl.ds(head, 1), :]
+    gain_k = gains[pl.ds(HEADS + head, 1), :]
+    tile_row = lax.broadcasted_iota(jnp.int32, (count, TILE, size), 1)
+    tails = received[:, TILE : 2 * TILE, :].astype(jnp.float32)
+    tails = tails[:, 0:1, :] + tails[:, 1:2, :]
+    tails = jnp.concatenate([jnp.zeros((1, 1, size), jnp.float32), tails[:-1]], axis=0)
+    pooled = received[:, 0:TILE, :].astype(jnp.float32)
+    pooled = jnp.where(tile_row == 0, (pooled + tails) * (1.0 / SHORTEN), pooled)
+    values = pooled.reshape(rows, size).astype(jnp.bfloat16)
+    pooled = values.astype(jnp.float32)
+    q = (pooled * gain_q).astype(jnp.bfloat16)
+    k = (pooled * gain_k).astype(jnp.bfloat16)
+    incoming_f = received[:, 2 * TILE : 3 * TILE, :].astype(jnp.float32).reshape(rows, size)
+    incoming = incoming_f.astype(jnp.bfloat16)
+    q_pos, k_pos = iotas(rows, rows)
+    scores = jnp.where(k_pos <= q_pos, mm_nt(q, k) * temper, NEGATIVE)
+    weights = jnp.exp(scores - jnp.max(scores, axis=1, keepdims=True))
+    weights = weights / jnp.sum(weights, axis=1, keepdims=True)
+    grads = mm_nt(incoming, values)
+    dots = jnp.sum(weights * grads, axis=1, keepdims=True)
+    ds = (weights * (grads - dots)).astype(jnp.bfloat16)
+    grad_q = mm(ds, k) * temper
+    grad_k = mm_tn(ds, q) * temper
+    grad_v = mm_tn(weights.astype(jnp.bfloat16), incoming)
+    grad = incoming_f + grad_q * gain_q + grad_k * gain_k + grad_v
+    sum_q = jnp.sum(grad_q * pooled, axis=0, keepdims=True)
+    sum_k = jnp.sum(grad_k * pooled, axis=0, keepdims=True)
+    gain = jnp.where(copy == 0, sum_q, sum_k)
+    gain_high = gain.astype(jnp.bfloat16).astype(jnp.float32)
+    gain_low = gain - gain_high
+    half = TILE // COPIES
+    grad = grad.reshape(count, TILE, size)
+    following = jnp.concatenate([grad[1:, 0:1, :], jnp.zeros((1, 1, size), jnp.float32)], axis=0)
+    later = jnp.where(tile_row == half, following, jnp.roll(grad, -half, axis=1))
+    block = jnp.where(copy == 0, grad, later)
+    block = jnp.where(tile_row == half + 1, gain_high[None], block)
+    block = jnp.where(tile_row == half + 2, gain_low[None], block)
+    block = jnp.where(tile_row == half + 3, 0.0, block)
+    send[...] = block.astype(jnp.bfloat16)
+
+
+def backward_kernel(tokens, prior, grad_output, gains, received, returned, partial, send, sums):
+    rows, width = tokens.shape
+    size = width // HEADS
+    temper = size ** (-0.5)
+    half = TILE // COPIES
+    q_pos, k_pos = iotas(rows, rows)
+    own_allowed = k_pos <= q_pos
+    prior_allowed = (k_pos > q_pos) & (chain_index() > 0)
+    row, column = iotas(rows, 2 * TILE)
+    short = (row + SHORTEN - 1) // SHORTEN
+    short = jnp.where(short > half, short + (TILE - half), short)
+    spread = (short == column).astype(jnp.bfloat16)
+    for head in range(HEADS):
+        part = slice(head * size, (head + 1) * size)
+        gain_q, gain_k = gains[0:1, part], gains[1:2, part]
+        own = tokens[:, part]
+        before = prior[:, part]
+        x = own.astype(jnp.float32)
+        x_before = before.astype(jnp.float32)
+        q = (x * gain_q).astype(jnp.bfloat16)
+        k = (x * gain_k).astype(jnp.bfloat16)
+        k_before = (x_before * gain_k).astype(jnp.bfloat16)
+        own_scores = jnp.where(own_allowed, mm_nt(q, k) * temper, NEGATIVE)
+        prior_scores = jnp.where(prior_allowed, mm_nt(q, k_before) * temper, NEGATIVE)
+        high = jnp.maximum(
+            jnp.max(own_scores, axis=1, keepdims=True), jnp.max(prior_scores, axis=1, keepdims=True)
+        )
+        own_w = jnp.exp(own_scores - high)
+        prior_w = jnp.exp(prior_scores - high)
+        inverse = 1.0 / (
+            jnp.sum(own_w, axis=1, keepdims=True) + jnp.sum(prior_w, axis=1, keepdims=True)
+        )
+        own_w = own_w * inverse
+        prior_w = prior_w * inverse
+        grad_pooled = received[head * COPIES : (head + 1) * COPIES].reshape(2 * TILE, size)
+        grad_mixed = grad_output[:, part].astype(jnp.float32) + mm(spread, grad_pooled) * (
+            1.0 / SHORTEN
+        )
+        incoming = grad_mixed.astype(jnp.bfloat16)
+        own_dw = mm_nt(incoming, own)
+        prior_dw = mm_nt(incoming, before)
+        dots = jnp.sum(own_w * own_dw + prior_w * prior_dw, axis=1, keepdims=True)
+        own_ds = (own_w * (own_dw - dots)).astype(jnp.bfloat16)
+        prior_ds = (prior_w * (prior_dw - dots)).astype(jnp.bfloat16)
+        grad_q = (mm(own_ds, k) + mm(prior_ds, k_before)) * temper
+        own_gk = mm_tn(own_ds, q) * temper
+        prior_gk = mm_tn(prior_ds, q) * temper
+        own_gv = mm_tn(own_w.astype(jnp.bfloat16), incoming)
+        prior_gv = mm_tn(prior_w.astype(jnp.bfloat16), incoming)
+        returned[:, part] = (prior_gk * gain_k + prior_gv).astype(jnp.bfloat16)
+        partial[:, part] = grad_mixed + grad_q * gain_q + own_gk * gain_k + own_gv
+        sums[head : head + 1, :] = jnp.sum(grad_q * x, axis=0, keepdims=True)
+        sums[HEADS + head : HEADS + head + 1, :] = jnp.sum(
+            own_gk * x + prior_gk * x_before, axis=0, keepdims=True
+        )
+    block = sums[...].astype(jnp.bfloat16)
+    for device in range(send.shape[0]):
+        send[device] = block
+
+
+def final_kernel(partial, arriving, received, short, grad_tokens, gain_grads, *, scale):
+    size = received.shape[-1]
+    half = TILE // COPIES
+    grad_tokens[...] = (partial[...] + arriving[...].astype(jnp.float32)).astype(jnp.bfloat16)
+    sums = jnp.sum(received[...].astype(jnp.float32), axis=0) * scale
+    for head in range(HEADS):
+        part = slice(head * size, (head + 1) * size)
+        gain_grads[0:1, part] = sums[head : head + 1]
+        gain_grads[1:2, part] = sums[HEADS + head : HEADS + head + 1]
+        for copy in range(COPIES):
+            block = short[head * COPIES + copy].astype(jnp.float32)
+            total = block[half + 1 : half + 2] + block[half + 2 : half + 3]
+            gain_grads[2 + copy : 3 + copy, part] = total * scale
+
+
+def call(kernel, outputs, flops, scratch=()):
+    return pl.pallas_call(
+        kernel,
+        out_shape=outputs,
+        scratch_shapes=list(scratch),
+        cost_estimate=pl.CostEstimate(flops=flops, bytes_accessed=1 << 20, transcendentals=1 << 19),
+    )
+
+
+def exchange(value):
+    return lax.all_to_all(value, CHAIN, split_axis=0, concat_axis=0, tiled=True)
+
+
+def head_shards(tokens, grad_output, query_gain, key_gain, short_query_gain, short_key_gain):
+    rows, width = tokens.shape
+    size = width // HEADS
+    count = lax.axis_size(CHAIN)
+    array = jax.ShapeDtypeStruct
+    low, full = jnp.bfloat16, jnp.float32
+    product = 2 * rows * rows * width
+    gains = jnp.stack([query_gain, key_gain])
+    short_gains = jnp.stack([short_query_gain, short_key_gain]).reshape(2 * HEADS, size)
+    prior = shifted_2(tokens, CHAIN, 1)
+    own_out, peak, total, grad_short = call(
+        own_kernel,
+        [
+            array((rows, width), full),
+            array((rows, size), full),
+            array((rows, size), full),
+            array((HEADS, rows // SHORTEN, size), low),
+        ],
+        2 * product,
+    )(tokens, grad_output, gains)
+    send = call(prior_kernel, array((count, 3 * TILE, size), low), 2 * product)(
+        tokens, prior, gains, own_out, peak, total, grad_short
+    )
+    back = call(short_kernel, array((count, TILE, size), low), 10 * (count * TILE) ** 2 * size)(
+        exchange(send), short_gains
+    )
+    back = exchange(back)
+    returned, partial, sums = call(
+        backward_kernel,
+        [
+            array((rows, width), low),
+            array((rows, width), full),
+            array((count, 2 * HEADS, size), low),
+        ],
+        10 * product,
+        [pltpu.VMEM((2 * HEADS, size), full)],
+    )(tokens, prior, grad_output, gains, back)
+    arriving = shifted_2(returned, CHAIN, -1)
+    sums = exchange(sums)
+    return call(
+        functools.partial(final_kernel, scale=(rows * count) ** (-0.5)),
+        [array((rows, width), low), array((4, width), full)],
+        0,
+    )(partial, arriving, sums, back)
 
 
 def head_scores(queries, key_rows):
@@ -250,8 +525,9 @@
 
 
 def solution(mesh):
+    paired = mesh.size == COPIES * HEADS
     return jax.shard_map(
-        shards,
+        head_shards if paired else shards,
         mesh=mesh,
         in_specs=(P(("grp", "seq"), None), P(("grp", "seq"), None), P(), P(), P(), P()),
         out_specs=(P(("grp", "seq"), None), P()),

time: 235 us -> 79 us (0.34)
  blocking collectives: 135 us -> 25.5 us
  local copies, waits for them, and re-layouts: 33.7 us -> 2.93 us
  Pallas kernels: 0 us -> 25.1 us
  other arithmetic: 18 us -> 1.35 us
  matrix products: 15.6 us -> 0 us
  starting transfers between devices: 28.7 us -> 14.7 us
  waiting for transfers between devices: 1.51 us -> 8.15 us
    all_gather x6 -> x0, blocking collectives: 82.4 us -> none  [the longest x1 14.2 us: shards(): fetched_keys = lax.all_gather(short_keys, 'seq', axis=0, tiled=True)]
    psum x1 -> x0, blocking collectives: 44 us -> none  [shards(): lax.psum(jnp.stack([grad_query_gain, grad_key_gain, grad_short_query, gra...]
    pallas_call x0 -> x5, Pallas kernels: none -> 25.1 us  [the longest x1 11.2 us: head_shards(): call(backward_kernel, [array((rows, width), low), array((rows, width), fu...]
    all_to_all x1 -> x2, blocking collectives: 8.75 us -> 25.5 us  [exchange(): return lax.all_to_all(value, CHAIN, split_axis=0, concat_axis=0, tiled=True)]
    dot_general x12 -> x0, matrix products: 15.6 us -> none  [the longest x1 3.6 us: shards(): jnp.einsum('qhe,khe->hqk', incoming_heads, value_heads, preferred_element...]
    slice x9 -> x0, local copies, waits for them, and re-layouts: 12.4 us -> none  [the longest x2 5.16 us: shards(): returned = full_gk[:WINDOW] * key_gain + full_gv[:WINDOW]]
    reduce_sum x5 -> x0, other arithmetic: 8.56 us -> none  [the longest x1 3.04 us: shards(): grad_query_gain = jnp.sum(local_gq * token_f, axis=0)]
    all_to_all x2 -> x1, waiting for transfers between devices: 0.01 us -> 8.15 us  [exchange(): return lax.all_to_all(value, CHAIN, split_axis=0, concat_axis=0, tiled=True)]
  transfers between devices with their start and end apart: 6 -> 3, of which waited for: 1 -> 1; matrix products, arithmetic and copies ran while one was open for 11% -> 3% of each run, Pallas kernels for 0% -> 4%
where the time goes in v1:
time: 79 us; the launch traced here: 78.4 us
  blocking collectives  25.5 us (32%)
  Pallas kernels  25.1 us (32%)
  starting transfers between devices  14.7 us (19%)
  waiting for transfers between devices  8.15 us (10%)
  local copies, waits for them, and re-layouts  2.93 us (4%)
  other arithmetic  1.35 us (2%)
    all_to_all x2, blocking collectives, exchange(): return lax.all_to_all(value, CHAIN, split_axis=0, concat_axis=0, tiled=True)  25.5 us
    pallas_call x1, Pallas kernels, head_shards(): call(backward_kernel, [array((rows, width), low), array((rows, width), fu...  11.2 us
    all_to_all x1, starting transfers between devices, exchange(): return lax.all_to_all(value, CHAIN, split_axis=0, concat_axis=0, tiled=True)  11 us
    all_to_all x1, waiting for transfers between devices, exchange(): return lax.all_to_all(value, CHAIN, split_axis=0, concat_axis=0, tiled=True)  8.15 us
    pallas_call x1, Pallas kernels, head_shards(): call(prior_kernel, array((count, 3 * TILE, size), low), 2 * product)  6.06 us
    ppermute x2, starting transfers between devices, shifted_2(): lax.ppermute(value, axis, [(source, source + steps) for source in range(l...  3.71 us
    pallas_call x1, Pallas kernels, head_shards(): call(own_kernel, [array((rows, width), full), array((rows, size), full),...  3.23 us
    unnamed x10, local copies, waits for them, and re-layouts  2.31 us
  transfers between devices with their start and end apart: 3, of which 1 were waited for; matrix products, arithmetic and copies ran while one was open for 3% of the time, Pallas kernels for 4%

profile of v1, /device:TPU:0, one launch (start us, length us, event | category | flops | bytes accessed | tf_op | source)
XLA Modules:
  0.0 78.4 jit_solution(9584859889618115893)
XLA Ops:
  0.6 2.4 %collective-permute-start = (bf16[128,2048]{1,0:T(8,128)(2,1)}, bf16[128,2048]{1,0:T(8,128)(2,1)S(1)}, u32[]{:S(2)}, u32[]{:S(2)}) collective-permute-start(bf16[128,2048]{1,0:T(8,128)(2,1)} %tokens.5), channel_id=1, source_target_pairs={{0,1},{1,2},{2,3},{3,4},{4,5},{5,6},{6,7},{7,8},{8,9},{9,10},{10,1... | collective-permute-start | bytes 1572872 | tf_op jit(solution)/shard_map/ppermute | solution.py:24
  3.1 1.3 %pad_maximum_fusion.gains = f32[2,2048]{1,0:T(2,128)} fusion(f32[1,2048]{1,0:T(1,128)} %bitcast.4, f32[1,2048]{1,0:T(1,128)} %bitcast.5), kind=kLoop, calls=%fused_computation | loop fusion | flops 4096 | bytes 32768 | tf_op jit(solution)/shard_map/stack | solution.py:256
  4.4 3.2 %shard_map.77 = (f32[128,2048]{1,0:T(8,128)}, f32[128,128]{1,0:T(8,128)}, f32[128,128]{1,0:T(8,128)}, bf16[16,8,128]{2,1,0:T(8,128)(2,1)}) custom-call(bf16[128,2048]{1,0:T(8,128)(2,1)} %tokens.5, bf16[128,2048]{1,0:T(8,128)(2,1)} %grad_output.3, f32[2,2048]{1,0:T(2,128)} %pad_maximum_fusion.gains), custom_call_target="tpu_custom_call" | custom-call | flops 134217728 | bytes 1048576 | tf_op jit(solution)/shard_map/pallas_call | solution.py:259
  7.6 0.0 collective-permute-done.prior
  7.6 0.0 copy-start
  7.6 0.8 %copy-done = bf16[128,2048]{1,0:T(8,128)(2,1)} copy-done((bf16[128,2048]{1,0:T(8,128)(2,1)}, bf16[128,2048]{1,0:T(8,128)(2,1)S(1)}, u32[]{:S(2)}) %copy-start) | copy-done | bytes 524312
  8.4 6.1 %shard_map.78 = bf16[32,24,128]{2,1,0:T(8,128)(2,1)} custom-call(bf16[128,2048]{1,0:T(8,128)(2,1)} %tokens.5, bf16[128,2048]{1,0:T(8,128)(2,1)} %copy-done, f32[2,2048]{1,0:T(2,128)} %pad_maximum_fusion.gains, f32[128,2048]{1,0:T(8,128)} %get-tuple-element.9.out, f32[128,128]{1,0:T(8,128)} %get-tuple-element.10.peak, f32[128,128]{1,0:T(8,128)} %get-tuple-element.11.total, ...), custom_call_target="tpu_custom_call" | custom-call | flops 134217728 | bytes 1048576 | tf_op jit(solution)/shard_map/pallas_call | solution.py:269
  14.5 0.0 copy-start.3
  14.5 0.0 copy-start.4
  14.5 11.0 %all-to-all-start = ((bf16[32,24,128]{2,1,0:T(8,128)(2,1)}), bf16[32,24,128]{2,1,0:T(8,128)(2,1)S(1)}, u32[]{:S(2)}, u32[]{:S(2)}) async-start(bf16[32,24,128]{2,1,0:T(8,128)(2,1)} %shard_map.78), calls=%async_computation | async-start | bytes 393216 | tf_op jit(solution)/shard_map/all_to_all | solution.py:246
  25.5 0.0 copy-done.3
  25.5 0.0 copy-done.4
  25.6 0.6 reshape.7.gains
  26.2 8.1 %all-to-all-done.received = bf16[32,24,128]{2,1,0:T(8,128)(2,1)S(1)} async-done(((bf16[32,24,128]{2,1,0:T(8,128)(2,1)}), bf16[32,24,128]{2,1,0:T(8,128)(2,1)S(1)}, u32[]{:S(2)}, u32[]{:S(2)}) %all-to-all-start) | async-done | bytes 196640 | tf_op jit(solution)/shard_map/all_to_all | solution.py:246
  34.4 0.0 copy-start.2
  34.4 0.7 copy-done.2
  35.0 2.3 %shard_map.79 = bf16[32,8,128]{2,1,0:T(8,128)(2,1)} custom-call(bf16[32,24,128]{2,1,0:T(8,128)(2,1)} %copy-done.2, f32[32,128]{1,0:T(8,128)} %reshape.7.gains), custom_call_target="tpu_custom_call" | custom-call | flops 83886080 | bytes 1048576 | tf_op jit(solution)/shard_map/pallas_call | solution.py:272
  37.3 10.6 %all_to_all.15.received.short = bf16[32,8,128]{2,1,0:T(8,128)(2,1)} all-to-all(bf16[32,8,128]{2,1,0:T(8,128)(2,1)} %shard_map.79), channel_id=1, replica_groups=mesh['grp'=4,'seq'=8] {'grp','seq'}, dimensions={0} | all-to-all | bytes 131072 | tf_op jit(solution)/shard_map/all_to_all | solution.py:246
  48.0 11.2 %shard_map.80 = (bf16[128,2048]{1,0:T(8,128)(2,1)}, f32[128,2048]{1,0:T(8,128)}, bf16[32,32,128]{2,1,0:T(8,128)(2,1)}) custom-call(bf16[128,2048]{1,0:T(8,128)(2,1)} %tokens.5, bf16[128,2048]{1,0:T(8,128)(2,1)} %copy-done, bf16[128,2048]{1,0:T(8,128)(2,1)} %grad_output.3, f32[2,2048]{1,0:T(2,128)} %pad_maximum_fusion.gains, ...), custom_call_target="tpu_custom_call" | custom-call | flops 671088640 | bytes 1048576 | tf_op jit(solution)/shard_map/pallas_call | solution.py:276
  59.1 1.3 %collective-permute-start.1 = (bf16[128,2048]{1,0:T(8,128)(2,1)}, bf16[128,2048]{1,0:T(8,128)(2,1)S(1)}, u32[]{:S(2)}, u32[]{:S(2)}) collective-permute-start(bf16[128,2048]{1,0:T(8,128)(2,1)} %get-tuple-element.14), channel_id=1, source_target_pairs={{1,0},{2,1},{3,2},{4,3},{5,4},{6,5},{7,6},{8,7},{9,8},{10,9},{11,1... | collective-permute-start | bytes 1572872 | tf_op jit(solution)/shard_map/ppermute | solution.py:24
  60.4 14.9 %all_to_all.16.received = bf16[32,32,128]{2,1,0:T(8,128)(2,1)} all-to-all(bf16[32,32,128]{2,1,0:T(8,128)(2,1)} %get-tuple-element.15), channel_id=1, replica_groups=mesh['grp'=4,'seq'=8] {'grp','seq'}, dimensions={0} | all-to-all | bytes 524288 | tf_op jit(solution)/shard_map/all_to_all | solution.py:246
  75.3 0.0 collective-permute-done.1.arriving
  75.3 0.8 %copy-done.1 = bf16[128,2048]{1,0:T(8,128)(2,1)} copy-done((bf16[128,2048]{1,0:T(8,128)(2,1)}, bf16[128,2048]{1,0:T(8,128)(2,1)S(1)}, u32[]{:S(2)}) %copy-start.1) | copy-done | bytes 524312
  76.1 2.3 %shard_map.81 = (bf16[128,2048]{1,0:T(8,128)(2,1)}, f32[4,2048]{1,0:T(4,128)}) custom-call(f32[128,2048]{1,0:T(8,128)} %get-tuple-element.13.partial, bf16[128,2048]{1,0:T(8,128)(2,1)} %copy-done.1, bf16[32,32,128]{2,1,0:T(8,128)(2,1)} %all_to_all.16.received, bf16[32,8,128]{2,1,0:T(8,128)(2,1)} %all_to_all.15.received.short), custom_call_target="tpu_custom_call" | custom-call | bytes 1048576 | tf_op jit(solution)/shard_map/pallas_call | solution.py:288
  (2 shorter events, 0.0 us)
Async XLA Ops:
  0.6 7.0 %collective-permute-start = (bf16[128,2048]{1,0:T(8,128)(2,1)}, bf16[128,2048]{1,0:T(8,128)(2,1)S(1)}, u32[]{:S(2)}, u32[]{:S(2)}) collective-permute-start(bf16[128,2048]{1,0:T(8,128)(2,1)} %tokens.5), channel_id=1, source_target_pairs={{0,1},{1,2},{2,3},{3,4},{4,5},{5,6},{6,7},{7,8},{8,9},{9,10},{10,1... | collective-permute-start | bytes 1572872 | tf_op jit(solution)/shard_map/ppermute | solution.py:24
  7.6 0.8 %copy-start = (bf16[128,2048]{1,0:T(8,128)(2,1)}, bf16[128,2048]{1,0:T(8,128)(2,1)S(1)}, u32[]{:S(2)}) copy-start(bf16[128,2048]{1,0:T(8,128)(2,1)S(1)} %collective-permute-done.prior) | copy-start | bytes 1572868
  14.5 11.0 %copy-start.3 = (f32[2048]{0:T(1024)S(1)}, f32[2048]{0:T(1024)}, u32[]{:S(2)}) copy-start(f32[2048]{0:T(1024)} %param.11) | copy-start | bytes 24580
  14.5 11.1 %copy-start.4 = (f32[2048]{0:T(1024)S(1)}, f32[2048]{0:T(1024)}, u32[]{:S(2)}) copy-start(f32[2048]{0:T(1024)} %param.10) | copy-start | bytes 24580
  14.5 19.9 %all-to-all-start = ((bf16[32,24,128]{2,1,0:T(8,128)(2,1)}), bf16[32,24,128]{2,1,0:T(8,128)(2,1)S(1)}, u32[]{:S(2)}, u32[]{:S(2)}) async-start(bf16[32,24,128]{2,1,0:T(8,128)(2,1)} %shard_map.78), calls=%async_computation | async-start | bytes 393216 | tf_op jit(solution)/shard_map/all_to_all | solution.py:246
  34.4 0.7 copy-start.2
  59.1 16.2 %collective-permute-start.1 = (bf16[128,2048]{1,0:T(8,128)(2,1)}, bf16[128,2048]{1,0:T(8,128)(2,1)S(1)}, u32[]{:S(2)}, u32[]{:S(2)}) collective-permute-start(bf16[128,2048]{1,0:T(8,128)(2,1)} %get-tuple-element.14), channel_id=1, source_target_pairs={{1,0},{2,1},{3,2},{4,3},{5,4},{6,5},{7,6},{8,7},{9,8},{10,9},{11,1... | collective-permute-start | bytes 1572872 | tf_op jit(solution)/shard_map/ppermute | solution.py:24
  75.3 0.8 %copy-start.1 = (bf16[128,2048]{1,0:T(8,128)(2,1)}, bf16[128,2048]{1,0:T(8,128)(2,1)S(1)}, u32[]{:S(2)}) copy-start(bf16[128,2048]{1,0:T(8,128)(2,1)S(1)} %collective-permute-done.1.arriving) | copy-start | bytes 1572868

commit v2 on v1

--- a/solution.py
+++ b/solution.py
@@ -13,6 +13,7 @@
 
 
 NEGATIVE = -1e30
+LOG2_E = 1.4426950408889634
 CHAIN = ("grp", "seq")
 TILE = 8
 COPIES = 2
@@ -47,58 +48,86 @@
     return lax.axis_index("grp") * lax.axis_size("seq") + lax.axis_index("seq")
 
 
-def own_kernel(tokens, grad_output, gains, out, peak, total, grad_short):
+def staggered(work):
+    active = []
+    waiting = list(range(HEADS))
+    while waiting or active:
+        if waiting:
+            active.append(work(waiting.pop(0)))
+        active = [item for item in active if next(item, True) is None]
+
+
+def raised(scores, high, size):
+    return jnp.exp2((scores - high) * (size ** (-0.5) * LOG2_E))
+
+
+def own_kernel(
+    tokens, grad_output, query_gain, key_gain, weights, peak, total, queries, grad_short
+):
     rows, width = tokens.shape
     size = width // HEADS
-    temper = size ** (-0.5)
-    q_pos, k_pos = iotas(rows, rows)
+    k_pos, q_pos = iotas(rows, rows)
     allowed = k_pos <= q_pos
     short, row = iotas(rows // SHORTEN, rows)
     pool = (row // SHORTEN == short).astype(jnp.bfloat16)
-    lane = lax.broadcasted_iota(jnp.int32, (rows, size), 1)
-    peaks = jnp.zeros((rows, size), jnp.float32)
-    totals = jnp.zeros((rows, size), jnp.float32)
-    for head in range(HEADS):
+
+    def work(head):
         part = slice(head * size, (head + 1) * size)
-        low = tokens[:, part]
-        x = low.astype(jnp.float32)
-        q = (x * gains[0:1, part]).astype(jnp.bfloat16)
-        k = (x * gains[1:2, part]).astype(jnp.bfloat16)
-        scores = jnp.where(allowed, mm_nt(q, k) * temper, NEGATIVE)
-        high = jnp.max(scores, axis=1, keepdims=True)
-        weights = jnp.exp(scores - high)
-        out[:, part] = mm(weights.astype(jnp.bfloat16), low)
-        peaks = jnp.where(lane == head, high, peaks)
-        totals = jnp.where(lane == head, jnp.sum(weights, axis=1, keepdims=True), totals)
+        x = tokens[:, part].astype(jnp.float32)
+        q = (x * query_gain[:, part]).astype(jnp.bfloat16)
+        k = (x * key_gain[:, part]).astype(jnp.bfloat16)
+        queries[:, part] = q
+        scores = jnp.where(allowed, mm_nt(k, q), NEGATIVE)
         grad_short[head] = mm(pool, grad_output[:, part]).astype(jnp.bfloat16)
-    peak[...] = peaks
-    total[...] = totals
-
-
-def prior_kernel(tokens, prior, gains, out, peak, total, grad_short, send):
+        yield
+        high = jnp.max(scores, axis=0, keepdims=True)
+        peak[head : head + 1, :] = high
+        yield
+        own = raised(scores, high, size)
+        weights[head] = own
+        total[head : head + 1, :] = jnp.sum(own, axis=0, keepdims=True)
+
+    staggered(work)
+
+
+def prior_kernel(
+    tokens, prior, key_gain, queries, own_weights, peak, total, grad_short, send, weights
+):
     rows, width = tokens.shape
     size = width // HEADS
-    temper = size ** (-0.5)
-    q_pos, k_pos = iotas(rows, rows)
+    k_pos, q_pos = iotas(rows, rows)
     allowed = (k_pos > q_pos) & (chain_index() > 0)
     short, row = iotas(2 * TILE, rows)
     pool = ((row + SHORTEN - 1) // SHORTEN == short).astype(jnp.bfloat16)
     tile_row = lax.broadcasted_iota(jnp.int32, (TILE, size), 0)
-    for head in range(HEADS):
+
+    def work(head):
         part = slice(head * size, (head + 1) * size)
-        x = tokens[:, part].astype(jnp.float32)
-        low = prior[:, part]
-        q = (x * gains[0:1, part]).astype(jnp.bfloat16)
-        k = (low.astype(jnp.float32) * gains[1:2, part]).astype(jnp.bfloat16)
-        scores = jnp.where(allowed, mm_nt(q, k) * temper, NEGATIVE)
-        own_high = peak[:, head : head + 1]
-        high = jnp.maximum(jnp.max(scores, axis=1, keepdims=True), own_high)
-        weights = jnp.exp(scores - high)
-        fade = jnp.exp(own_high - high)
-        sums = total[:, head : head + 1] * fade + jnp.sum(weights, axis=1, keepdims=True)
-        local = (out[:, part] * fade + mm(weights.astype(jnp.bfloat16), low)) / sums
-        mixed = (x + local).astype(jnp.bfloat16)
+        before = prior[:, part]
+        k = (before.astype(jnp.float32) * key_gain[:, part]).astype(jnp.bfloat16)
+        scores = jnp.where(allowed, mm_nt(k, queries[:, part]), NEGATIVE)
+        yield
+        own_high = peak[head : head + 1, :]
+        high = jnp.maximum(jnp.max(scores, axis=0, keepdims=True), own_high)
+        yield
+        prior_w = raised(scores, high, size)
+        fade = raised(own_high, high, size)
+        scale = 1.0 / (jnp.sum(prior_w, axis=0, keepdims=True) + total[head : head + 1, :] * fade)
+        yield
+        both = jnp.concatenate(
+            [
+                (prior_w * scale).astype(jnp.bfloat16),
+                (own_weights[head] * (fade * scale)).astype(jnp.bfloat16),
+            ],
+            axis=0,
+        )
+        weights[head] = both
+        own = tokens[:, part]
+        local = mm_tn(both, jnp.concatenate([before, own], axis=0))
+        yield
+        mixed = (own.astype(jnp.float32) + local).astype(jnp.bfloat16)
         pooled = mm(pool, mixed)
+        yield
         rows_sent = jnp.where(tile_row == 0, pooled[:TILE], pooled[:TILE] * (1.0 / SHORTEN))
         tail = pooled[TILE:]
         tail_high = tail.astype(jnp.bfloat16).astype(jnp.float32)
@@ -109,16 +138,17 @@
             send[head * COPIES + copy, TILE : 2 * TILE, :] = tail_rows.astype(jnp.bfloat16)
             send[head * COPIES + copy, 2 * TILE : 3 * TILE, :] = grad_short[head]
 
-
-def short_kernel(received, gains, send):
+    staggered(work)
+
+
+def short_kernel(received, query_gain, key_gain, send):
     count, _, size = received.shape
     rows = count * TILE
     temper = size ** (-0.5)
     me = chain_index()
-    head = me // COPIES
     copy = me % COPIES
-    gain_q = gains[pl.ds(head, 1), :]
-    gain_k = gains[pl.ds(HEADS + head, 1), :]
+    part = pl.ds(pl.multiple_of(me // COPIES * size, size), size)
+    gain_q, gain_k = query_gain[:, part], key_gain[:, part]
     tile_row = lax.broadcasted_iota(jnp.int32, (count, TILE, size), 1)
     tails = received[:, TILE : 2 * TILE, :].astype(jnp.float32)
     tails = tails[:, 0:1, :] + tails[:, 1:2, :]
@@ -131,16 +161,16 @@
     k = (pooled * gain_k).astype(jnp.bfloat16)
     incoming_f = received[:, 2 * TILE : 3 * TILE, :].astype(jnp.float32).reshape(rows, size)
     incoming = incoming_f.astype(jnp.bfloat16)
-    q_pos, k_pos = iotas(rows, rows)
-    scores = jnp.where(k_pos <= q_pos, mm_nt(q, k) * temper, NEGATIVE)
-    weights = jnp.exp(scores - jnp.max(scores, axis=1, keepdims=True))
-    weights = weights / jnp.sum(weights, axis=1, keepdims=True)
-    grads = mm_nt(incoming, values)
-    dots = jnp.sum(weights * grads, axis=1, keepdims=True)
+    k_pos, q_pos = iotas(rows, rows)
+    scores = jnp.where(k_pos <= q_pos, mm_nt(k, q) * temper, NEGATIVE)
+    weights = jnp.exp(scores - jnp.max(scores, axis=0, keepdims=True))
+    weights = weights * (1.0 / jnp.sum(weights, axis=0, keepdims=True))
+    grads = mm_nt(values, incoming)
+    dots = jnp.sum(weights * grads, axis=0, keepdims=True)
     ds = (weights * (grads - dots)).astype(jnp.bfloat16)
-    grad_q = mm(ds, k) * temper
-    grad_k = mm_tn(ds, q) * temper
-    grad_v = mm_tn(weights.astype(jnp.bfloat16), incoming)
+    grad_q = mm_tn(ds, k) * temper
+    grad_k = mm(ds, q) * temper
+    grad_v = mm(weights.astype(jnp.bfloat16), incoming)
     grad = incoming_f + grad_q * gain_q + grad_k * gain_k + grad_v
     sum_q = jnp.sum(grad_q * pooled, axis=0, keepdims=True)
     sum_k = jnp.sum(grad_k * pooled, axis=0, keepdims=True)
@@ -158,62 +188,62 @@
     send[...] = block.astype(jnp.bfloat16)
 
 
-def backward_kernel(tokens, prior, grad_output, gains, received, returned, partial, send, sums):
+def backward_kernel(
+    tokens,
+    prior,
+    grad_output,
+    query_gain,
+    key_gain,
+    weights,
+    received,
+    returned,
+    partial,
+    send,
+    sums,
+):
     rows, width = tokens.shape
     size = width // HEADS
     temper = size ** (-0.5)
     half = TILE // COPIES
-    q_pos, k_pos = iotas(rows, rows)
-    own_allowed = k_pos <= q_pos
-    prior_allowed = (k_pos > q_pos) & (chain_index() > 0)
     row, column = iotas(rows, 2 * TILE)
     short = (row + SHORTEN - 1) // SHORTEN
     short = jnp.where(short > half, short + (TILE - half), short)
-    spread = (short == column).astype(jnp.bfloat16)
-    for head in range(HEADS):
+    spread = jnp.where(short == column, 1.0 / SHORTEN, 0.0).astype(jnp.bfloat16)
+
+    def work(head):
         part = slice(head * size, (head + 1) * size)
-        gain_q, gain_k = gains[0:1, part], gains[1:2, part]
-        own = tokens[:, part]
-        before = prior[:, part]
-        x = own.astype(jnp.float32)
-        x_before = before.astype(jnp.float32)
-        q = (x * gain_q).astype(jnp.bfloat16)
-        k = (x * gain_k).astype(jnp.bfloat16)
-        k_before = (x_before * gain_k).astype(jnp.bfloat16)
-        own_scores = jnp.where(own_allowed, mm_nt(q, k) * temper, NEGATIVE)
-        prior_scores = jnp.where(prior_allowed, mm_nt(q, k_before) * temper, NEGATIVE)
-        high = jnp.maximum(
-            jnp.max(own_scores, axis=1, keepdims=True), jnp.max(prior_scores, axis=1, keepdims=True)
+        grad_pooled = received[head * COPIES : (head + 1) * COPIES].reshape(2 * TILE, size)
+        grad_mixed = grad_output[:, part].astype(jnp.float32) + mm(spread, grad_pooled)
+        incoming = grad_mixed.astype(jnp.bfloat16)
+        partial[:, part] = grad_mixed
+        yield
+        context = jnp.concatenate([prior[:, part], tokens[:, part]], axis=0)
+        dw = mm_nt(context, incoming)
+        yield
+        w_low = weights[head]
+        w = w_low.astype(jnp.float32)
+        dots = jnp.sum(w * dw, axis=0, keepdims=True)
+        yield
+        ds = (w * (dw - dots)).astype(jnp.bfloat16)
+        context_f = context.astype(jnp.float32)
+        x = context_f[rows:]
+        k = (context_f * key_gain[:, part]).astype(jnp.bfloat16)
+        q = x * query_gain[:, part]
+        scaled_q = (q * (key_gain[:, part] * temper)).astype(jnp.bfloat16)
+        yield
+        pair = mm_tn(ds, jnp.concatenate([k, context], axis=1))
+        grad_kv = mm(
+            jnp.concatenate([ds, w_low], axis=1), jnp.concatenate([scaled_q, incoming], axis=0)
         )
-        own_w = jnp.exp(own_scores - high)
-        prior_w = jnp.exp(prior_scores - high)
-        inverse = 1.0 / (
-            jnp.sum(own_w, axis=1, keepdims=True) + jnp.sum(prior_w, axis=1, keepdims=True)
-        )
-        own_w = own_w * inverse
-        prior_w = prior_w * inverse
-        grad_pooled = received[head * COPIES : (head + 1) * COPIES].reshape(2 * TILE, size)
-        grad_mixed = grad_output[:, part].astype(jnp.float32) + mm(spread, grad_pooled) * (
-            1.0 / SHORTEN
-        )
-        incoming = grad_mixed.astype(jnp.bfloat16)
-        own_dw = mm_nt(incoming, own)
-        prior_dw = mm_nt(incoming, before)
-        dots = jnp.sum(own_w * own_dw + prior_w * prior_dw, axis=1, keepdims=True)
-        own_ds = (own_w * (own_dw - dots)).astype(jnp.bfloat16)
-        prior_ds = (prior_w * (prior_dw - dots)).astype(jnp.bfloat16)
-        grad_q = (mm(own_ds, k) + mm(prior_ds, k_before)) * temper
-        own_gk = mm_tn(own_ds, q) * temper
-        prior_gk = mm_tn(prior_ds, q) * temper
-        own_gv = mm_tn(own_w.astype(jnp.bfloat16), incoming)
-        prior_gv = mm_tn(prior_w.astype(jnp.bfloat16), incoming)
-        returned[:, part] = (prior_gk * gain_k + prior_gv).astype(jnp.bfloat16)
-        partial[:, part] = grad_mixed + grad_q * gain_q + own_gk * gain_k + own_gv
+        yield
+        grad_q, mixed_k = pair[:, :size], pair[:, size:]
+        returned[:, part] = grad_kv[:rows].astype(jnp.bfloat16)
+        partial[:, part] += grad_q * (query_gain[:, part] * temper) + grad_kv[rows:]
         sums[head : head + 1, :] = jnp.sum(grad_q * x, axis=0, keepdims=True)
-        sums[HEADS + head : HEADS + head + 1, :] = jnp.sum(
-            own_gk * x + prior_gk * x_before, axis=0, keepdims=True
-        )
-    block = sums[...].astype(jnp.bfloat16)
+        sums[HEADS + head : HEADS + head + 1, :] = jnp.sum(mixed_k * q, axis=0, keepdims=True)
+
+    staggered(work)
+    block = (sums[...] * temper).astype(jnp.bfloat16)
     for device in range(send.shape[0]):
         send[device] = block
 
@@ -238,6 +268,7 @@
         kernel,
         out_shape=outputs,
         scratch_shapes=list(scratch),
+        compiler_params=pltpu.CompilerParams(vmem_limit_bytes=24 << 20),
         cost_estimate=pl.CostEstimate(flops=flops, bytes_accessed=1 << 20, transcendentals=1 << 19),
     )
 
@@ -253,24 +284,29 @@
     array = jax.ShapeDtypeStruct
     low, full = jnp.bfloat16, jnp.float32
     product = 2 * rows * rows * width
-    gains = jnp.stack([query_gain, key_gain])
-    short_gains = jnp.stack([short_query_gain, short_key_gain]).reshape(2 * HEADS, size)
+    query_gain, key_gain, short_query_gain, short_key_gain = (
+        gain.reshape(1, width)
+        for gain in (query_gain, key_gain, short_query_gain, short_key_gain)
+    )
     prior = shifted_2(tokens, CHAIN, 1)
-    own_out, peak, total, grad_short = call(
+    own_weights, peak, total, queries, grad_short = call(
         own_kernel,
         [
-            array((rows, width), full),
-            array((rows, size), full),
-            array((rows, size), full),
+            array((HEADS, rows, rows), full),
+            array((HEADS, rows), full),
+            array((HEADS, rows), full),
+            array((rows, width), low),
             array((HEADS, rows // SHORTEN, size), low),
         ],
-        2 * product,
-    )(tokens, grad_output, gains)
-    send = call(prior_kernel, array((count, 3 * TILE, size), low), 2 * product)(
-        tokens, prior, gains, own_out, peak, total, grad_short
-    )
+        product,
+    )(tokens, grad_output, query_gain, key_gain)
+    send, weights = call(
+        prior_kernel,
+        [array((count, 3 * TILE, size), low), array((HEADS, 2 * rows, rows), low)],
+        3 * product,
+    )(tokens, prior, key_gain, queries, own_weights, peak, total, grad_short)
     back = call(short_kernel, array((count, TILE, size), low), 10 * (count * TILE) ** 2 * size)(
-        exchange(send), short_gains
+        exchange(send), short_query_gain, short_key_gain
     )
     back = exchange(back)
     returned, partial, sums = call(
@@ -280,9 +316,9 @@
             array((rows, width), full),
             array((count, 2 * HEADS, size), low),
         ],
-        10 * product,
+        8 * product,
         [pltpu.VMEM((2 * HEADS, size), full)],
-    )(tokens, prior, grad_output, gains, back)
+    )(tokens, prior, grad_output, query_gain, key_gain, weights, back)
     arriving = shifted_2(returned, CHAIN, -1)
     sums = exchange(sums)
     return call(
@@ -525,9 +561,13 @@
 
 
 def solution(mesh):
-    paired = mesh.size == COPIES * HEADS
+    def program(tokens, *others):
+        rows = tokens.shape[0]
+        paired = mesh.size == COPIES * HEADS and rows == WINDOW == SHORTEN * TILE
+        return (head_shards if paired else shards)(tokens, *others)
+
     return jax.shard_map(
-        head_shards if paired else shards,
+        program,
         mesh=mesh,
         in_specs=(P(("grp", "seq"), None), P(("grp", "seq"), None), P(), P(), P(), P()),
         out_specs=(P(("grp", "seq"), None), P()),

time: 79 us -> 60.5 us (0.77)
  blocking collectives: 25.5 us -> 44.4 us
  Pallas kernels: 25.1 us -> 7.7 us
  starting transfers between devices: 14.7 us -> 3.72 us
  waiting for transfers between devices: 8.15 us -> 0.01 us
  other arithmetic: 1.35 us -> 0 us
    all_to_all x2 -> x3, blocking collectives: 25.5 us -> 44.4 us  [exchange(): return lax.all_to_all(value, CHAIN, split_axis=0, concat_axis=0, tiled=True)]
    all_to_all x1 -> x0, starting transfers between devices: 11 us -> none  [exchange(): return lax.all_to_all(value, CHAIN, split_axis=0, concat_axis=0, tiled=True)]
    all_to_all x1 -> x0, waiting for transfers between devices: 8.15 us -> none  [exchange(): return lax.all_to_all(value, CHAIN, split_axis=0, concat_axis=0, tiled=True)]
    pallas_call x1, Pallas kernels: 11.2 us -> 3.22 us  [head_shards(): call(backward_kernel, [array((rows, width), low), array((rows, width), fu...]
    pallas_call x2, Pallas kernels: 9.29 us -> 2.95 us  [the longest x1 2.26 us: head_shards(): call(prior_kernel, [array((count, 3 * TILE, size), low), array((HEADS, 2...]
    pallas_call x1, Pallas kernels: 2.3 us -> 0.65 us  [head_shards(): call(short_kernel, array((count, TILE, size), low), 10 * (count * TILE) *...]
    pallas_call x1, Pallas kernels: 2.31 us -> 0.89 us  [head_shards(): call(functools.partial(final_kernel, scale=(rows * count) ** (-0.5)), [ar...]
    another operation x2 -> x0, other arithmetic: 1.35 us -> none  [the longest x1 1.33 us: head_shards(): gains = jnp.stack([query_gain, key_gain])]
  transfers between devices with their start and end apart: 3 -> 2, of which waited for: 1 -> 0; matrix products, arithmetic and copies ran while one was open for 3% -> 0% of each run, Pallas kernels for 4% -> 1%
where the time goes in v2:
time: 60.5 us; the launch traced here: 60 us
  blocking collectives  44.4 us (73%)
  Pallas kernels  7.7 us (13%)
  starting transfers between devices  3.72 us (6%)
  local copies, waits for them, and re-layouts  3.49 us (6%)
  between operations  0.7 us (1%)
    all_to_all x3, blocking collectives, exchange(): return lax.all_to_all(value, CHAIN, split_axis=0, concat_axis=0, tiled=True)  44.4 us
    ppermute x2, starting transfers between devices, shifted_2(): lax.ppermute(value, axis, [(source, source + steps) for source in range(l...  3.72 us
    unnamed x16, local copies, waits for them, and re-layouts  3.49 us
    pallas_call x1, Pallas kernels, head_shards(): call(backward_kernel, [array((rows, width), low), array((rows, width), fu...  3.22 us
    pallas_call x1, Pallas kernels, head_shards(): call(prior_kernel, [array((count, 3 * TILE, size), low), array((HEADS, 2...  2.26 us
  transfers between devices with their start and end apart: 2, of which 0 were waited for; matrix products, arithmetic and copies ran while one was open for 0% of the time, Pallas kernels for 1%

profile of v2, /device:TPU:0, one launch (start us, length us, event | category | flops | bytes accessed | tf_op | source)
XLA Modules:
  0.0 60.0 jit_solution(14310278548702707870)
XLA Ops:
  0.6 2.4 %collective-permute-start = (bf16[128,2048]{1,0:T(8,128)(2,1)}, bf16[128,2048]{1,0:T(8,128)(2,1)S(1)}, u32[]{:S(2)}, u32[]{:S(2)}) collective-permute-start(bf16[128,2048]{1,0:T(8,128)(2,1)} %tokens.5), channel_id=1, source_target_pairs={{0,1},{1,2},{2,3},{3,4},{4,5},{5,6},{6,7},{7,8},{8,9},{9,10},{10,1... | collective-permute-start | bytes 1572872 | tf_op jit(solution)/shard_map/ppermute | solution.py:25
  3.1 0.0 copy-start
  3.1 1.0 %copy-done = bf16[128,2048]{1,0:T(8,128)(2,1)S(1)} copy-done((bf16[128,2048]{1,0:T(8,128)(2,1)S(1)}, bf16[128,2048]{1,0:T(8,128)(2,1)}, u32[]{:S(2)}) %copy-start) | copy-done | bytes 524312
  4.1 0.0 copy-start.2
  4.1 1.0 %copy-done.2 = bf16[128,2048]{1,0:T(8,128)(2,1)S(1)} copy-done((bf16[128,2048]{1,0:T(8,128)(2,1)S(1)}, bf16[128,2048]{1,0:T(8,128)(2,1)}, u32[]{:S(2)}) %copy-start.2) | copy-done | bytes 524312
  5.2 0.7 %copy-done.4 = f32[2048]{0:T(1024)S(1)} copy-done((f32[2048]{0:T(1024)S(1)}, f32[2048]{0:T(1024)}, u32[]{:S(2)}) %copy-start.4) | copy-done | bytes 8216
  5.9 0.0 copy-start.5
  5.9 0.7 %copy-done.5 = f32[2048]{0:T(1024)S(1)} copy-done((f32[2048]{0:T(1024)S(1)}, f32[2048]{0:T(1024)}, u32[]{:S(2)}) %copy-start.5) | copy-done | bytes 8216
  6.6 0.7 %shard_map.77 = (f32[16,128,128]{2,1,0:T(8,128)S(1)}, f32[16,128]{1,0:T(8,128)S(1)}, f32[16,128]{1,0:T(8,128)S(1)}, bf16[128,2048]{1,0:T(8,128)(2,1)S(1)}, bf16[16,8,128]{2,1,0:T(8,128)(2,1)S(1)}) custom-call(bf16[128,2048]{1,0:T(8,128)(2,1)S(1)} %copy-done, bf16[128,2048]{1,0:T(8,128)(2,1)S(1)} %copy-done.2, f32[1,2048]{1,0:T(1,128)S(1)} %bitcast.7, ...), custom_call_target="tpu_custom_call" | custom-call | flops 67108864 | bytes 1048576 | tf_op jit(solution)/shard_map/pallas_call | solution.py:292
  7.2 0.0 collective-permute-done.prior
  7.2 2.3 %shard_map.78 = (bf16[32,24,128]{2,1,0:T(8,128)(2,1)S(1)}, bf16[16,256,128]{2,1,0:T(8,128)(2,1)S(1)}) custom-call(bf16[128,2048]{1,0:T(8,128)(2,1)S(1)} %copy-done, bf16[128,2048]{1,0:T(8,128)(2,1)S(1)} %collective-permute-done.prior, f32[1,2048]{1,0:T(1,128)S(1)} %bitcast.5, bf16[128,2048]{1,0:T(8,128)(2,1)S(1)} %get-tuple-element.12.queries, ...), custom_call_target="tpu_custom_call" | custom-call | flops 201326592 | bytes 1048576 | tf_op jit(solution)/shard_map/pallas_call | solution.py:303
  9.5 0.0 copy-start.7
  9.5 20.0 %all_to_all.15.received = bf16[32,24,128]{2,1,0:T(8,128)(2,1)S(1)} all-to-all(bf16[32,24,128]{2,1,0:T(8,128)(2,1)S(1)} %get-tuple-element.18), channel_id=1, replica_groups=mesh['grp'=4,'seq'=8] {'grp','seq'}, dimensions={0} | all-to-all | bytes 393216 | tf_op jit(solution)/shard_map/all_to_all | solution.py:277
  29.6 0.0 copy-done.6
  29.6 0.0 copy-done.7
  29.6 0.6 %shard_map.79 = bf16[32,8,128]{2,1,0:T(8,128)(2,1)S(1)} custom-call(bf16[32,24,128]{2,1,0:T(8,128)(2,1)S(1)} %all_to_all.15.received, f32[1,2048]{1,0:T(1,128)S(1)} %bitcast.9, f32[1,2048]{1,0:T(1,128)S(1)} %bitcast.10), custom_call_target="tpu_custom_call" | custom-call | flops 83886080 | bytes 1048576 | tf_op jit(solution)/shard_map/pallas_call | solution.py:308
  30.2 9.8 %all_to_all.16.received.short = bf16[32,8,128]{2,1,0:T(8,128)(2,1)S(1)} all-to-all(bf16[32,8,128]{2,1,0:T(8,128)(2,1)S(1)} %shard_map.79), channel_id=1, replica_groups=mesh['grp'=4,'seq'=8] {'grp','seq'}, dimensions={0} | all-to-all | bytes 131072 | tf_op jit(solution)/shard_map/all_to_all | solution.py:277
  40.0 0.0 copy-done.1
  40.0 0.0 copy-done.3
  40.1 3.2 %shard_map.80 = (bf16[128,2048]{1,0:T(8,128)(2,1)S(1)}, f32[128,2048]{1,0:T(8,128)S(1)}, bf16[32,32,128]{2,1,0:T(8,128)(2,1)S(1)}) custom-call(bf16[128,2048]{1,0:T(8,128)(2,1)S(1)} %copy-done.1, bf16[128,2048]{1,0:T(8,128)(2,1)S(1)} %collective-permute-done.prior, bf16[128,2048]{1,0:T(8,128)(2,1)S(1)} %copy-done.3, f32[1,2048]{1,0:T(1,128)S(1)} %bitcast.8, ...), custom_call_target="tpu_custom_call" | custom-call | flops 536870912 | bytes 1048576 | tf_op jit(solution)/shard_map/pallas_call | solution.py:312
  43.3 1.3 %collective-permute-start.1 = (bf16[128,2048]{1,0:T(8,128)(2,1)S(1)}, bf16[128,2048]{1,0:T(8,128)(2,1)S(1)}, u32[]{:S(2)}, u32[]{:S(2)}) collective-permute-start(bf16[128,2048]{1,0:T(8,128)(2,1)S(1)} %get-tuple-element.20), channel_id=1, source_target_pairs={{1,0},{2,1},{3,2},{4,3},{5,4},{6,5},{7,6},{8,7},{9,8},{10,9},{11,1... | collective-permute-start | bytes 1572872 | tf_op jit(solution)/shard_map/ppermute | solution.py:25
  44.6 14.6 %all_to_all.17.received = bf16[32,32,128]{2,1,0:T(8,128)(2,1)S(1)} all-to-all(bf16[32,32,128]{2,1,0:T(8,128)(2,1)S(1)} %get-tuple-element.21), channel_id=1, replica_groups=mesh['grp'=4,'seq'=8] {'grp','seq'}, dimensions={0} | all-to-all | bytes 524288 | tf_op jit(solution)/shard_map/all_to_all | solution.py:277
  59.1 0.0 collective-permute-done.1.arriving
  59.1 0.9 %shard_map.81 = (bf16[128,2048]{1,0:T(8,128)(2,1)}, f32[4,2048]{1,0:T(4,128)}) custom-call(f32[128,2048]{1,0:T(8,128)S(1)} %get-tuple-element.19.partial, bf16[128,2048]{1,0:T(8,128)(2,1)S(1)} %collective-permute-done.1.arriving, bf16[32,32,128]{2,1,0:T(8,128)(2,1)S(1)} %all_to_all.17.received, bf16[32,8,128]{2,1,0:T(8,128)(2,1)S(1)} %all_to_all.16.received.short), custom_call_target="tpu_custom_call" | custom-call | bytes 1048576 | tf_op jit(solution)/shard_map/pallas_call | solution.py:324
  (4 shorter events, 0.0 us)
Async XLA Ops:
  0.6 6.6 %collective-permute-start = (bf16[128,2048]{1,0:T(8,128)(2,1)}, bf16[128,2048]{1,0:T(8,128)(2,1)S(1)}, u32[]{:S(2)}, u32[]{:S(2)}) collective-permute-start(bf16[128,2048]{1,0:T(8,128)(2,1)} %tokens.5), channel_id=1, source_target_pairs={{0,1},{1,2},{2,3},{3,4},{4,5},{5,6},{6,7},{7,8},{8,9},{9,10},{10,1... | collective-permute-start | bytes 1572872 | tf_op jit(solution)/shard_map/ppermute | solution.py:25
  3.1 1.0 %copy-start = (bf16[128,2048]{1,0:T(8,128)(2,1)S(1)}, bf16[128,2048]{1,0:T(8,128)(2,1)}, u32[]{:S(2)}) copy-start(bf16[128,2048]{1,0:T(8,128)(2,1)} %tokens.5) | copy-start | bytes 1572868
  4.1 1.0 %copy-start.2 = (bf16[128,2048]{1,0:T(8,128)(2,1)S(1)}, bf16[128,2048]{1,0:T(8,128)(2,1)}, u32[]{:S(2)}) copy-start(bf16[128,2048]{1,0:T(8,128)(2,1)} %grad_output.3) | copy-start | bytes 1572868
  5.2 0.7 %copy-start.4 = (f32[2048]{0:T(1024)S(1)}, f32[2048]{0:T(1024)}, u32[]{:S(2)}) copy-start(f32[2048]{0:T(1024)} %param.9) | copy-start | bytes 24580
  5.9 0.7 %copy-start.5 = (f32[2048]{0:T(1024)S(1)}, f32[2048]{0:T(1024)}, u32[]{:S(2)}) copy-start(f32[2048]{0:T(1024)} %param.8) | copy-start | bytes 24580
  9.5 20.1 %copy-start.6 = (f32[2048]{0:T(1024)S(1)}, f32[2048]{0:T(1024)}, u32[]{:S(2)}) copy-start(f32[2048]{0:T(1024)} %param.10) | copy-start | bytes 24580
  9.5 20.1 %copy-start.7 = (f32[2048]{0:T(1024)S(1)}, f32[2048]{0:T(1024)}, u32[]{:S(2)}) copy-start(f32[2048]{0:T(1024)} %param.11) | copy-start | bytes 24580
  29.6 10.5 %copy-start.1 = (bf16[128,2048]{1,0:T(8,128)(2,1)S(1)}, bf16[128,2048]{1,0:T(8,128)(2,1)}, u32[]{:S(2)}) copy-start(bf16[128,2048]{1,0:T(8,128)(2,1)} %tokens.5) | copy-start | bytes 1572868
  29.6 10.5 %copy-start.3 = (bf16[128,2048]{1,0:T(8,128)(2,1)S(1)}, bf16[128,2048]{1,0:T(8,128)(2,1)}, u32[]{:S(2)}) copy-start(bf16[128,2048]{1,0:T(8,128)(2,1)} %grad_output.3) | copy-start | bytes 1572868
  43.3 15.9 %collective-permute-start.1 = (bf16[128,2048]{1,0:T(8,128)(2,1)S(1)}, bf16[128,2048]{1,0:T(8,128)(2,1)S(1)}, u32[]{:S(2)}, u32[]{:S(2)}) collective-permute-start(bf16[128,2048]{1,0:T(8,128)(2,1)S(1)} %get-tuple-element.20), channel_id=1, source_target_pairs={{1,0},{2,1},{3,2},{4,3},{5,4},{6,5},{7,6},{8,7},{9,8},{10,9},{11,1... | collective-permute-start | bytes 1572872 | tf_op jit(solution)/shard_map/ppermute | solution.py:25
